TPU v7x, 32 devices: a whole 2x2x4 slice. The times are simulated.
32 devices in a mesh: sub: 8 (over z, x), scen: 4 (over y, core).
Axes of the slice: x: 2, y: 2, z: 4, core: 2. Of those that a mesh axis runs over, the one named last changes fastest.
Arguments:
- internal_inverse: bfloat16 [32, 1024, 1024], P('sub', 'scen')
- schur_inverse: bfloat16 [512, 512], P('sub')
- port_nodes: int32 [32, 16], P('sub'), may hold values from 0 to 1023, as said below
- turbine_count: int32 [8], P('sub'), may hold values from 1 to 4, as said below
- partner_port: int32 [512], P('sub'), may hold values from 0 to 511, as said below
- cable_delay: int32 [512], P('sub'), may hold values from 2 to 4, as said below
- history_w: bfloat16 [4, 256, 512], P(None, 'scen', 'sub'), may hold values from -6 to 6
- node_state: float32 [256, 32, 1024], P('scen', 'sub'), may hold values from -6 to 6
- node_gain: float32 [32, 1024], P('sub'), may hold values from 0.02 to 0.3
- stroke_node: int32 [256], P('scen'), may hold values from 0 to 32767, as said below
- stroke_amp: float32 [256], P('scen'), may hold values from 3 to 30
Outputs:
- node_voltage: bfloat16 [256, 32, 1024], P('scen', 'sub')
- cable_waves: bfloat16 [3, 256, 512], P(None, 'scen', 'sub')
Inputs may be any that keep to these rules, and one draw needn't show every extreme that they name: `port_nodes`: the 16 nodes named for one slot are distinct. `turbine_count`: the turbines of one index of sub fill its first slots; the busiest hold all 4. `partner_port`: a cable joins two ports that name each other, of a turbine and the next turbine in slot order (the next used slot, on the same or the next index of sub); a port that names itself has no cable. `cable_delay`: both ends of a cable carry the same delay. `stroke_node`: slot times 1024 plus local node; a stroke on an empty slot injects nothing.
All inputs are finite; a program needn't handle non-finite values.
Results may differ from a plain program's by a relative error of at most 0.004.
The roundings to bfloat16 on the way count: a program that leaves them out, or rounds other values in their place, can miss the bound.
Values may be sent and summed in bfloat16 or wider, within the bound.
A program may use at most 64 MiB of HBM per device.

v0:
```python
import math
import jax
import jax.numpy as jnp
from jax import lax
from jax.sharding import PartitionSpec as P

STEPS = 3


def padded(block, sides, width):
    for axis, dim in sides:
        count = lax.axis_size(axis)
        forward = [(i, i + 1) for i in range(count - 1)]
        backward = [(target, source) for source, target in forward]
        low = lax.ppermute(
            lax.slice_in_dim(block, block.shape[dim] - width, None, axis=dim), axis, forward
        )
        high = lax.ppermute(lax.slice_in_dim(block, 0, width, axis=dim), axis, backward)
        block = jnp.concatenate([low, block, high], axis=dim)
    return block


def per_device(
    internal_inverse,
    schur_inverse,
    port_nodes,
    turbine_count,
    partner_port,
    cable_delay,
    history_w,
    node_state,
    node_gain,
    stroke_node,
    stroke_amp,
):
    slot_count = port_nodes.shape[0]
    port_count = port_nodes.shape[1]
    node_count = internal_inverse.shape[2]
    scen_rows = node_state.shape[0]
    depth = history_w.shape[0]
    if_dev = slot_count * port_count
    device = lax.axis_index("sub")
    slot_used = (jnp.arange(slot_count, dtype=jnp.int32) < turbine_count[0]).astype(jnp.float32)
    port_used = jnp.repeat(slot_used, port_count)
    node_range = jnp.arange(node_count, dtype=jnp.int32)
    port_hot = (port_nodes[:, :, None] == node_range[None, None, :]).astype(jnp.float32)
    node_ids = (device * slot_count + jnp.arange(slot_count, dtype=jnp.int32))[
        :, None
    ] * node_count + node_range[None, :]
    stroke_hot = (stroke_node[:, None, None] == node_ids[None]).astype(jnp.float32)
    own_ports = device * if_dev + jnp.arange(if_dev, dtype=jnp.int32)
    paired = (partner_port != own_ports).astype(jnp.float32)
    partner_col = partner_port - (device - 1) * if_dev
    history_wide = padded(history_w, (("sub", 2),), if_dev)
    hist_cols = jnp.take(history_wide, partner_col, axis=2).astype(jnp.float32)
    schur_wide = schur_inverse.astype(jnp.float32)
    full_inverse = lax.all_gather(internal_inverse, "scen", axis=1, tiled=True)
    port_rows = jnp.take_along_axis(full_inverse, port_nodes[:, :, None], axis=1)
    fresh_cols = jnp.zeros((scen_rows, if_dev), jnp.float32)
    companion = node_state
    wave_list = []
    voltage = jnp.zeros((scen_rows, slot_count, node_count), jnp.float32)
    for step_index in range(STEPS):
        time_now = step_index + 1
        lag_time = time_now - cable_delay
        picked = jnp.zeros((scen_rows, if_dev), jnp.float32)
        for delay_back in range(depth):
            picked = picked + jnp.where(
                (lag_time == -delay_back)[None, :], hist_cols[delay_back], 0.0
            )
        picked = picked + jnp.where((lag_time == 1)[None, :], fresh_cols, 0.0)
        cable_in = -picked * paired[None, :]
        inject = jnp.einsum(
            "sgp,gpn->sgn",
            cable_in.reshape(scen_rows, slot_count, port_count),
            port_hot,
            precision=lax.Precision.HIGHEST,
        )
        wave_value = math.exp(-0.3 * time_now) - math.exp(-2.0 * time_now)
        strike = (stroke_amp * wave_value)[:, None, None] * stroke_hot
        injected = (slot_used[None, :, None] * (companion + strike + inject)).astype(jnp.bfloat16)
        opened = jnp.einsum(
            "sgm,gmn->sgn", injected, full_inverse, preferred_element_type=jnp.float32
        )
        port_open = jnp.take_along_axis(opened, port_nodes[None], axis=2).reshape(scen_rows, if_dev)
        every_port = lax.all_gather(port_open, "sub", axis=1, tiled=True)
        link_current = lax.dot_general(
            every_port,
            schur_wide,
            (((1,), (1,)), ((), ())),
            precision=lax.Precision.HIGHEST,
            preferred_element_type=jnp.float32,
        )
        link_half = link_current.astype(jnp.bfloat16).reshape(scen_rows, slot_count, port_count)
        correction = jnp.einsum(
            "sgp,gpn->sgn", link_half, port_rows, preferred_element_type=jnp.float32
        )
        voltage = slot_used[None, :, None] * (opened - correction)
        companion = -companion - 2.0 * node_gain[None] * voltage
        port_volt = jnp.take_along_axis(voltage, port_nodes[None], axis=2).reshape(
            scen_rows, if_dev
        )
        outgoing = (port_used[None, :] * (0.5 * port_volt + cable_in)).astype(jnp.bfloat16)
        wave_list.append(outgoing)
        if step_index == 0:
            fresh_wide = padded(outgoing, (("sub", 1),), if_dev)
            fresh_cols = jnp.take(fresh_wide, partner_col, axis=1).astype(jnp.float32)
    return (voltage.astype(jnp.bfloat16), jnp.stack(wave_list))


def solution(mesh):
    return jax.shard_map(
        per_device,
        mesh=mesh,
        in_specs=(
            P("sub", "scen", None),
            P("sub", None),
            P("sub", None),
            P("sub"),
            P("sub"),
            P("sub"),
            P(None, "scen", "sub"),
            P("scen", "sub", None),
            P("sub", None),
            P("scen"),
            P("scen"),
        ),
        out_specs=(P("scen", "sub", None), P(None, "scen", "sub")),
        check_vma=False,
    )
```

profile of v0, /device:TPU:0, one launch (start us, length us, event | category | flops | bytes accessed | tf_op | source)
XLA Modules:
  0.0 228.1 jit_solution(14548788545594329199)
XLA Ops:
  7.3 0.7 all-gather.2.cloned.1.call-update
  8.1 0.1 copy.44
  8.2 4.8 %collective-permute-start = (bf16[4,64,64]{1,0,2:T(4,128)(2,1)S(1)}, bf16[4,64,64]{1,0,2:T(4,128)(2,1)S(1)}, u32[]{:S(2)}, u32[]{:S(2)}) collective-permute-start(bf16[4,64,64]{1,0,2:T(4,128)(2,1)S(1)} %copy.44), channel_id=1, source_target_pairs={{0,4},{4,8},{8,12},{12,16},{16,20},{20,24},{24,28},{1,5},{5,9},{9,... | collective-permute-start | bytes 98312 | tf_op jit(solution)/shard_map/ppermute | solution.py:15
  13.0 1.3 collective-permute-start.1
  15.2 0.6 broadcast_multiply_fusion.1
  16.0 0.6 broadcast_multiply_fusion
  17.0 0.1 reshape.565
  17.2 0.6 mul.248
  17.9 0.6 broadcast_in_dim.277
  18.5 0.6 broadcast_in_dim.267
  19.1 0.6 broadcast_in_dim.269
  19.6 0.7 broadcast_in_dim.271
  20.3 0.6 broadcast_in_dim.273
  20.9 0.6 broadcast_in_dim.275
  21.5 0.7 broadcast_in_dim.286
  22.2 0.6 broadcast_in_dim.288
  22.8 0.6 broadcast_in_dim.290
  23.4 0.6 broadcast_in_dim.292
  24.0 0.7 broadcast_in_dim.294
  24.7 0.2 pad_maximum_fusion
  24.9 0.7 gather_fusion
  25.6 0.1 convert_bitcast_fusion
  25.7 0.1 fusion.99
  25.9 1.3 fusion.12
  27.2 43.5 %all-gather.2.cloned.1.call-done = bf16[4,1024,1024]{2,1,0:T(8,128)(2,1)} async-done(((bf16[4,256,1024]{2,1,0:T(8,128)(2,1)}), bf16[4,1024,1024]{2,1,0:T(8,128)(2,1)}) %all-gather.2.cloned.1.call-update) | async-done | bytes 8388624 | tf_op jit(solution)/shard_map/all_gather | solution.py:57
  70.7 5.0 %convolution_bitcast_fusion.7 = f32[64,4,1024]{2,0,1:T(8,128)S(1)} fusion(bf16[64,4,1024]{2,0,1:T(8,128)(2,1)S(1)} %fusion.12, bf16[4,1024,1024]{2,1,0:T(8,128)(2,1)} %all-gather.2.cloned.1.call-done), kind=kOutput, calls=%fused_computation.29 | convolution fusion | flops 536870912 | bytes 9961472 | tf_op jit(solution)/shard_map/sgm,gmn->sgn/dot_general | solution.py:82
  75.8 1.9 copy.47
  77.8 1.5 gather_fusion.3
  79.3 30.8 %all_gather.13 = f32[64,512]{0,1:T(8,128)S(1)} all-gather(f32[64,64]{0,1:T(8,128)S(1)} %bitcast.170), channel_id=1, replica_groups=mesh['sub'=8,'scen'=4] {'sub'}, dimensions={1}, use_global_device_ids=true | all-gather | bytes 147456 | tf_op jit(solution)/shard_map/all_gather | solution.py:86
  110.1 0.4 convolution_convert_fusion.2
  110.5 0.1 copy.48
  110.6 1.8 gather_fusion.2
  112.4 0.4 fusion.9
  112.8 0.6 copy.49
  113.4 0.9 gather_fusion.4
  114.3 0.9 fusion.45
  115.3 3.4 %collective-permute-start.2 = (bf16[64,64]{0,1:T(8,128)(2,1)S(1)}, bf16[64,64]{0,1:T(8,128)(2,1)S(1)}, u32[]{:S(2)}, u32[]{:S(2)}) collective-permute-start(bf16[64,64]{0,1:T(8,128)(2,1)S(1)} %fusion.45), channel_id=1, source_target_pairs={{0,4},{4,8},{8,12},{12,16},{16,20},{20,24},{24,28},{1,5},{5,9},{9,... | collective-permute-start | bytes 24584 | tf_op jit(solution)/shard_map/ppermute | solution.py:15
  118.6 1.3 collective-permute-start.3
  119.9 2.0 multiply_convert_fusion.2
  121.9 2.3 %collective-permute-done.3 = bf16[64,64]{0,1:T(8,128)(2,1)S(1)} collective-permute-done((bf16[64,64]{0,1:T(8,128)(2,1)S(1)}, bf16[64,64]{0,1:T(8,128)(2,1)S(1)}, u32[]{:S(2)}, u32[]{:S(2)}) %collective-permute-start.3) | collective-permute-done | bytes 8224 | tf_op jit(solution)/shard_map/ppermute | solution.py:18
  124.3 0.8 gather_fusion.1
  125.0 2.8 %fusion.13 = bf16[64,4,1024]{2,0,1:T(8,128)(2,1)S(1)} fusion(f32[64]{0:T(128)} %get-tuple-element.35, s32[4,1024]{1,0:T(4,128)} %copy-done.14, f32[4]{0:T(128)} %copy-done.21, s32[64]{0:T(128)} %param.22, f32[64,4,1024]{2,0,1:T(8,128)S(1)} %fusion.9, f32[4,1024]{1,0:T(4,128)} %broadcast_multiply_fusion, f32[64,4,1024]{2,1,0:T(4,128)} %param.20, ...), kind=kOutput, calls=%fused_computation.34 | convolution fusion | flops 52809728 | bytes 2729360 | tf_op jit(solution)/shard_map/sgp,gpn->sgn/dot_general | solution.py:73
  127.8 5.0 %convolution_bitcast_fusion.4 = f32[64,4,1024]{2,0,1:T(8,128)S(1)} fusion(bf16[64,4,1024]{2,0,1:T(8,128)(2,1)S(1)} %fusion.13, bf16[4,1024,1024]{2,1,0:T(8,128)(2,1)} %all-gather.2.cloned.1.call-done), kind=kOutput, calls=%fused_computation.22 | convolution fusion | flops 536870912 | bytes 9961472 | tf_op jit(solution)/shard_map/sgm,gmn->sgn/dot_general | solution.py:82
  132.8 1.9 copy.50
  134.8 1.5 gather_fusion.5
  136.3 30.9 %all_gather.14 = f32[64,512]{0,1:T(8,128)S(1)} all-gather(f32[64,64]{0,1:T(8,128)S(1)} %bitcast.171), channel_id=1, replica_groups=mesh['sub'=8,'scen'=4] {'sub'}, dimensions={1}, use_global_device_ids=true | all-gather | bytes 147456 | tf_op jit(solution)/shard_map/all_gather | solution.py:86
  167.2 0.4 convolution_convert_fusion.1
  167.7 1.0 fusion.5
  168.9 1.9 copy.54
  171.0 2.8 %fusion.14 = bf16[64,4,1024]{2,0,1:T(8,128)(2,1)S(1)} fusion(f32[64,4,1024]{2,0,1:T(8,128)S(1)} %fusion.5, f32[64]{0:T(128)S(1)} %copy-done.35, s32[4,1024]{1,0:T(4,128)S(1)} %copy-done.15, f32[4,1024]{1,0:T(4,128)S(1)} %copy-done.16, f32[4]{0:T(128)S(1)} %copy-done.22, s32[64]{0:T(128)S(1)} %copy-done.57, f32[64,4,1024]{2,0,1:T(8,128)S(1)} %fusion.9, ...), kind=kOutput, calls=%fused_computation.35 | convolution fusion | flops 53596160 | bytes 3777936 | tf_op jit(solution)/shard_map/sgp,gpn->sgn/dot_general | solution.py:73
  173.7 5.0 %convolution_bitcast_fusion.1 = f32[64,4,1024]{2,0,1:T(8,128)S(1)} fusion(bf16[64,4,1024]{2,0,1:T(8,128)(2,1)S(1)} %fusion.14, bf16[4,1024,1024]{2,1,0:T(8,128)(2,1)} %all-gather.2.cloned.1.call-done), kind=kOutput, calls=%fused_computation.15 | convolution fusion | flops 536870912 | bytes 9961472 | tf_op jit(solution)/shard_map/sgm,gmn->sgn/dot_general | solution.py:82
  178.7 0.6 copy.52
  179.4 0.9 gather_fusion.6
  180.3 30.7 %all_gather.15 = f32[64,512]{0,1:T(8,128)S(1)} all-gather(f32[64,64]{0,1:T(8,128)S(1)} %bitcast.172), channel_id=1, replica_groups=mesh['sub'=8,'scen'=4] {'sub'}, dimensions={1}, use_global_device_ids=true | all-gather | bytes 147456 | tf_op jit(solution)/shard_map/all_gather | solution.py:86
  211.0 0.4 convolution_convert_fusion
  211.5 1.2 fusion.100
  212.8 1.9 copy.57
  214.7 1.5 gather_fusion.8
  216.2 0.9 gather_fusion.7
  217.3 0.9 multiply_convert_fusion.1
  218.3 0.9 multiply_convert_fusion
  219.2 0.1 pad_maximum_fusion.1
  219.4 0.7 copy.59
  220.1 1.2 copy.58
  (161 shorter events, 1.7 us)
Async XLA Ops:
  7.2 103.0 %copy-start = (bf16[64,512]{1,0:T(8,128)(2,1)S(1)}, bf16[64,512]{1,0:T(8,128)(2,1)}, u32[]{:S(2)}) copy-start(bf16[64,512]{1,0:T(8,128)(2,1)} %param.14) | copy-start | bytes 196612
  7.2 7.8 %copy-start.65 = (s32[64]{0:T(128)S(1)}, s32[64]{0:T(128)}, u32[]{:S(2)}) copy-start(s32[64]{0:T(128)} %param.17) | copy-start | bytes 772
  7.2 7.8 %copy-start.66 = (s32[64]{0:T(128)S(1)}, s32[64]{0:T(128)}, u32[]{:S(2)}) copy-start(s32[64]{0:T(128)} %param.18) | copy-start | bytes 772
  7.2 8.0 %copy-start.64 = (f32[64]{0:T(128)S(1)}, f32[64]{0:T(128)}, u32[]{:S(2)}) copy-start(f32[64]{0:T(128)} %param.23) | copy-start | bytes 772
  7.2 8.6 %copy-start.18 = (s32[4,16]{1,0:T(4,128)S(1)}, s32[4,16]{1,0:T(4,128)}, u32[]{:S(2)}) copy-start(s32[4,16]{1,0:T(4,128)} %param.15) | copy-start | bytes 772
  7.2 8.7 %copy-start.19 = (f32[4,1024]{1,0:T(4,128)S(1)}, f32[4,1024]{1,0:T(4,128)}, u32[]{:S(2)}) copy-start(f32[4,1024]{1,0:T(4,128)} %param.21) | copy-start | bytes 49156
  7.2 18.6 %copy-start.3 = (f32[64,4,1024]{2,1,0:T(4,128)S(1)}, f32[64,4,1024]{2,1,0:T(4,128)}, u32[]{:S(2)}) copy-start(f32[64,4,1024]{2,1,0:T(4,128)} %param.20) | copy-start | bytes 3145732
  7.3 18.6 %copy-start.56 = (s32[64]{0:T(128)S(1)}, s32[64]{0:T(128)}, u32[]{:S(2)}) copy-start(s32[64]{0:T(128)} %param.22) | copy-start | bytes 772
  7.3 63.4 %all-gather.2.cloned.1.call-start = ((), (), s32[]{:S(2)}) async-start(), calls=%async_computation | async-start | bytes 10485760 | tf_op jit(solution)/shard_map/all_gather | solution.py:57
  8.2 16.5 %collective-permute-start = (bf16[4,64,64]{1,0,2:T(4,128)(2,1)S(1)}, bf16[4,64,64]{1,0,2:T(4,128)(2,1)S(1)}, u32[]{:S(2)}, u32[]{:S(2)}) collective-permute-start(bf16[4,64,64]{1,0,2:T(4,128)(2,1)S(1)} %copy.44), channel_id=1, source_target_pairs={{0,4},{4,8},{8,12},{12,16},{16,20},{20,24},{24,28},{1,5},{5,9},{9,... | collective-permute-start | bytes 98312 | tf_op jit(solution)/shard_map/ppermute | solution.py:15
  13.0 11.7 %collective-permute-start.1 = (bf16[4,64,64]{1,0,2:T(4,128)(2,1)S(1)}, bf16[4,64,64]{1,0,2:T(4,128)(2,1)S(1)}, u32[]{:S(2)}, u32[]{:S(2)}) collective-permute-start(bf16[4,64,64]{1,0,2:T(4,128)(2,1)S(1)} %copy.44), channel_id=1, source_target_pairs={{4,0},{8,4},{12,8},{16,12},{20,16},{24,20},{28,24},{5,1},{9,5},{13... | collective-permute-start | bytes 98312 | tf_op jit(solution)/shard_map/ppermute | solution.py:18
  15.1 10.5 %copy-start.40 = (pred[64]{0:T(512)(128)(4,1)}, pred[64]{0:T(512)(128)(4,1)S(1)}, u32[]{:S(2)}) copy-start(pred[64]{0:T(512)(128)(4,1)S(1)} %get-tuple-element.50) | copy-start | bytes 196
  15.1 10.5 %copy-start.42 = (pred[64]{0:T(512)(128)(4,1)}, pred[64]{0:T(512)(128)(4,1)S(1)}, u32[]{:S(2)}) copy-start(pred[64]{0:T(512)(128)(4,1)S(1)} %get-tuple-element.51) | copy-start | bytes 196
  15.1 10.5 %copy-start.44 = (pred[64]{0:T(512)(128)(4,1)}, pred[64]{0:T(512)(128)(4,1)S(1)}, u32[]{:S(2)}) copy-start(pred[64]{0:T(512)(128)(4,1)S(1)} %get-tuple-element.52) | copy-start | bytes 196
  15.1 10.5 %copy-start.46 = (pred[64]{0:T(512)(128)(4,1)}, pred[64]{0:T(512)(128)(4,1)S(1)}, u32[]{:S(2)}) copy-start(pred[64]{0:T(512)(128)(4,1)S(1)} %get-tuple-element.39) | copy-start | bytes 196
  15.1 10.5 %copy-start.48 = (pred[64]{0:T(512)(128)(4,1)}, pred[64]{0:T(512)(128)(4,1)S(1)}, u32[]{:S(2)}) copy-start(pred[64]{0:T(512)(128)(4,1)S(1)} %get-tuple-element.44) | copy-start | bytes 196
  15.1 10.5 %copy-start.50 = (pred[64]{0:T(512)(128)(4,1)}, pred[64]{0:T(512)(128)(4,1)S(1)}, u32[]{:S(2)}) copy-start(pred[64]{0:T(512)(128)(4,1)S(1)} %get-tuple-element.45) | copy-start | bytes 196
  15.1 10.5 %copy-start.52 = (pred[64]{0:T(512)(128)(4,1)}, pred[64]{0:T(512)(128)(4,1)S(1)}, u32[]{:S(2)}) copy-start(pred[64]{0:T(512)(128)(4,1)S(1)} %get-tuple-element.46) | copy-start | bytes 196
  15.1 10.5 %copy-start.54 = (pred[64]{0:T(512)(128)(4,1)}, pred[64]{0:T(512)(128)(4,1)S(1)}, u32[]{:S(2)}) copy-start(pred[64]{0:T(512)(128)(4,1)S(1)} %get-tuple-element.47) | copy-start | bytes 196
  15.1 60.6 %copy-start.24 = (pred[64]{0:T(512)(128)(4,1)}, pred[64]{0:T(512)(128)(4,1)S(1)}, u32[]{:S(2)}) copy-start(pred[64]{0:T(512)(128)(4,1)S(1)} %get-tuple-element.9) | copy-start | bytes 196
  15.1 60.6 %copy-start.32 = (pred[64]{0:T(512)(128)(4,1)}, pred[64]{0:T(512)(128)(4,1)S(1)}, u32[]{:S(2)}) copy-start(pred[64]{0:T(512)(128)(4,1)S(1)} %get-tuple-element.41) | copy-start | bytes 196
  15.2 60.6 %copy-start.33 = (pred[64]{0:T(512)(128)(4,1)}, pred[64]{0:T(512)(128)(4,1)S(1)}, u32[]{:S(2)}) copy-start(pred[64]{0:T(512)(128)(4,1)S(1)} %get-tuple-element.42) | copy-start | bytes 196
  15.2 60.6 %copy-start.34 = (pred[64]{0:T(512)(128)(4,1)}, pred[64]{0:T(512)(128)(4,1)S(1)}, u32[]{:S(2)}) copy-start(pred[64]{0:T(512)(128)(4,1)S(1)} %get-tuple-element.43) | copy-start | bytes 196
  15.2 60.6 %copy-start.36 = (pred[64]{0:T(512)(128)(4,1)}, pred[64]{0:T(512)(128)(4,1)S(1)}, u32[]{:S(2)}) copy-start(pred[64]{0:T(512)(128)(4,1)S(1)} %get-tuple-element.48) | copy-start | bytes 196
  15.2 60.6 %copy-start.38 = (pred[64]{0:T(512)(128)(4,1)}, pred[64]{0:T(512)(128)(4,1)S(1)}, u32[]{:S(2)}) copy-start(pred[64]{0:T(512)(128)(4,1)S(1)} %get-tuple-element.49) | copy-start | bytes 196
  15.2 60.5 %copy-start.30 = (s32[1024]{0:T(1024)}, s32[1024]{0:T(1024)S(1)}, u32[]{:S(2)}) copy-start(s32[1024]{0:T(1024)S(1)} %pad_clamp_fusion) | copy-start | bytes 12292
  15.9 96.5 %copy-start.28 = (pred[4,16]{1,0:T(4,128)(4,1)}, pred[4,16]{1,0:T(4,128)(4,1)S(1)}, u32[]{:S(2)}) copy-start(pred[4,16]{1,0:T(4,128)(4,1)S(1)} %compare_and_fusion) | copy-start | bytes 196
  16.0 59.8 %copy-start.14 = (s32[4,1024]{1,0:T(4,128)}, s32[4,1024]{1,0:T(4,128)S(1)}, u32[]{:S(2)}) copy-start(s32[4,1024]{1,0:T(4,128)S(1)} %iota_add_fusion) | copy-start | bytes 49156
  16.6 95.8 %copy-start.21 = (f32[4]{0:T(128)}, f32[4]{0:T(128)S(1)}, u32[]{:S(2)}) copy-start(f32[4]{0:T(128)S(1)} %compare_convert_fusion.1) | copy-start | bytes 52
  16.6 59.1 %copy-start.26 = (f32[4,16]{1,0:T(4,128)}, f32[4,16]{1,0:T(4,128)S(1)}, u32[]{:S(2)}) copy-start(f32[4,16]{1,0:T(4,128)S(1)} %mul.238) | copy-start | bytes 772
  25.8 50.0 %copy-start.4 = (f32[1,64,64]{1,0,2:T(1,128)}, f32[1,64,64]{1,0,2:T(1,128)S(1)}, u32[]{:S(2)}) copy-start(f32[1,64,64]{1,0,2:T(1,128)S(1)} %get-tuple-element.12) | copy-start | bytes 49156
  25.9 50.0 %copy-start.6 = (f32[1,64,64]{1,0,2:T(1,128)}, f32[1,64,64]{1,0,2:T(1,128)S(1)}, u32[]{:S(2)}) copy-start(f32[1,64,64]{1,0,2:T(1,128)S(1)} %get-tuple-element.13) | copy-start | bytes 49156
  25.9 49.9 %copy-start.8 = (f32[1,64,64]{1,0,2:T(1,128)}, f32[1,64,64]{1,0,2:T(1,128)S(1)}, u32[]{:S(2)}) copy-start(f32[1,64,64]{1,0,2:T(1,128)S(1)} %get-tuple-element.14) | copy-start | bytes 49156
  115.3 6.7 %collective-permute-start.2 = (bf16[64,64]{0,1:T(8,128)(2,1)S(1)}, bf16[64,64]{0,1:T(8,128)(2,1)S(1)}, u32[]{:S(2)}, u32[]{:S(2)}) collective-permute-start(bf16[64,64]{0,1:T(8,128)(2,1)S(1)} %fusion.45), channel_id=1, source_target_pairs={{0,4},{4,8},{8,12},{12,16},{16,20},{20,24},{24,28},{1,5},{5,9},{9,... | collective-permute-start | bytes 24584 | tf_op jit(solution)/shard_map/ppermute | solution.py:15
  118.6 5.6 %collective-permute-start.3 = (bf16[64,64]{0,1:T(8,128)(2,1)S(1)}, bf16[64,64]{0,1:T(8,128)(2,1)S(1)}, u32[]{:S(2)}, u32[]{:S(2)}) collective-permute-start(bf16[64,64]{0,1:T(8,128)(2,1)S(1)} %fusion.45), channel_id=1, source_target_pairs={{4,0},{8,4},{12,8},{16,12},{20,16},{24,20},{28,24},{5,1},{9,5},{13... | collective-permute-start | bytes 24584 | tf_op jit(solution)/shard_map/ppermute | solution.py:18
  125.0 7.8 %copy-start.10 = (bf16[64,64]{1,0:T(8,128)(2,1)}, bf16[64,64]{1,0:T(8,128)(2,1)S(1)}, u32[]{:S(2)}) copy-start(bf16[64,64]{1,0:T(8,128)(2,1)S(1)} %gather_fusion.1) | copy-start | bytes 24580
  168.7 2.1 copy-start.5
  168.7 2.1 copy-start.7
  168.7 2.1 copy-start.9
  168.8 2.1 copy-start.11
  168.8 2.1 copy-start.15
  168.8 2.1 copy-start.16
  168.8 2.1 copy-start.22
  168.8 2.1 copy-start.27
  168.8 2.1 copy-start.35
  168.8 2.1 copy-start.57
  178.7 32.8 %copy-start.23 = (f32[4]{0:T(128)S(1)}, f32[4]{0:T(128)}, u32[]{:S(2)}) copy-start(f32[4]{0:T(128)} %copy-done.21) | copy-start | bytes 52
  178.7 32.8 %copy-start.29 = (pred[4,16]{1,0:T(4,128)(4,1)S(1)}, pred[4,16]{1,0:T(4,128)(4,1)}, u32[]{:S(2)}) copy-start(pred[4,16]{1,0:T(4,128)(4,1)} %copy-done.28) | copy-start | bytes 196
  212.7 3.5 %copy-start.1 = (f32[64,4,1024]{0,2,1:T(8,128)S(1)}, f32[64,4,1024]{0,2,1:T(8,128)}, u32[]{:S(2)}) copy-start(f32[64,4,1024]{0,2,1:T(8,128)} %copy.54) | copy-start | bytes 3145732
  212.7 4.5 %copy-start.12 = (bf16[64,64]{1,0:T(8,128)(2,1)S(1)}, bf16[64,64]{1,0:T(8,128)(2,1)}, u32[]{:S(2)}) copy-start(bf16[64,64]{1,0:T(8,128)(2,1)} %copy-done.10) | copy-start | bytes 24580
  212.7 4.5 %copy-start.20 = (f32[64]{0:T(128)S(1)}, f32[64]{0:T(128)}, u32[]{:S(2)}) copy-start(f32[64]{0:T(128)} %mul.248) | copy-start | bytes 772
  212.7 4.5 %copy-start.25 = (pred[64]{0:T(512)(128)(4,1)S(1)}, pred[64]{0:T(512)(128)(4,1)}, u32[]{:S(2)}) copy-start(pred[64]{0:T(512)(128)(4,1)} %copy-done.24) | copy-start | bytes 196
  212.7 4.5 %copy-start.47 = (pred[64]{0:T(512)(128)(4,1)S(1)}, pred[64]{0:T(512)(128)(4,1)}, u32[]{:S(2)}) copy-start(pred[64]{0:T(512)(128)(4,1)} %copy-done.46) | copy-start | bytes 196
  212.7 4.5 %copy-start.49 = (pred[64]{0:T(512)(128)(4,1)S(1)}, pred[64]{0:T(512)(128)(4,1)}, u32[]{:S(2)}) copy-start(pred[64]{0:T(512)(128)(4,1)} %copy-done.48) | copy-start | bytes 196
  212.7 4.5 %copy-start.51 = (pred[64]{0:T(512)(128)(4,1)S(1)}, pred[64]{0:T(512)(128)(4,1)}, u32[]{:S(2)}) copy-start(pred[64]{0:T(512)(128)(4,1)} %copy-done.50) | copy-start | bytes 196
  212.7 4.5 %copy-start.53 = (pred[64]{0:T(512)(128)(4,1)S(1)}, pred[64]{0:T(512)(128)(4,1)}, u32[]{:S(2)}) copy-start(pred[64]{0:T(512)(128)(4,1)} %copy-done.52) | copy-start | bytes 196
  212.7 4.5 %copy-start.55 = (pred[64]{0:T(512)(128)(4,1)S(1)}, pred[64]{0:T(512)(128)(4,1)}, u32[]{:S(2)}) copy-start(pred[64]{0:T(512)(128)(4,1)} %copy-done.54) | copy-start | bytes 196
  214.7 3.5 %copy-start.37 = (pred[64]{0:T(512)(128)(4,1)S(1)}, pred[64]{0:T(512)(128)(4,1)}, u32[]{:S(2)}) copy-start(pred[64]{0:T(512)(128)(4,1)} %copy-done.36) | copy-start | bytes 196
  214.7 3.5 %copy-start.39 = (pred[64]{0:T(512)(128)(4,1)S(1)}, pred[64]{0:T(512)(128)(4,1)}, u32[]{:S(2)}) copy-start(pred[64]{0:T(512)(128)(4,1)} %copy-done.38) | copy-start | bytes 196
  214.7 3.5 %copy-start.41 = (pred[64]{0:T(512)(128)(4,1)S(1)}, pred[64]{0:T(512)(128)(4,1)}, u32[]{:S(2)}) copy-start(pred[64]{0:T(512)(128)(4,1)} %copy-done.40) | copy-start | bytes 196
  214.7 3.6 %copy-start.43 = (pred[64]{0:T(512)(128)(4,1)S(1)}, pred[64]{0:T(512)(128)(4,1)}, u32[]{:S(2)}) copy-start(pred[64]{0:T(512)(128)(4,1)} %copy-done.42) | copy-start | bytes 196
  214.7 3.6 %copy-start.45 = (pred[64]{0:T(512)(128)(4,1)S(1)}, pred[64]{0:T(512)(128)(4,1)}, u32[]{:S(2)}) copy-start(pred[64]{0:T(512)(128)(4,1)} %copy-done.44) | copy-start | bytes 196
  214.7 4.5 %copy-start.13 = (bf16[1,64,64]{1,0,2:T(2,128)(2,1)S(1)}, bf16[1,64,64]{1,0,2:T(2,128)(2,1)}, u32[]{:S(2)}) copy-start(bf16[1,64,64]{1,0,2:T(2,128)(2,1)} %multiply_convert_fusion.2) | copy-start | bytes 24580
  214.7 5.4 %copy-start.2 = (bf16[64,4,1024]{2,0,1:T(8,128)(2,1)S(1)}, bf16[64,4,1024]{2,0,1:T(8,128)(2,1)}, u32[]{:S(2)}) copy-start(bf16[64,4,1024]{2,0,1:T(8,128)(2,1)} %get-tuple-element.37) | copy-start | bytes 1572868
  (8 other events, 15.2 us)
Sparse Core Ops, SparseCore 0:
  9.7 60.9 all-gather.1
where the time goes:
time: 229 us; the launch traced here: 228 us
  blocking collectives  92.5 us (40%)
  waiting for transfers between devices  46.5 us (20%)
  local copies, waits for them, and re-layouts  30 us (13%)
  matrix products  25.5 us (11%)
  between operations  15.8 us (7%)
  starting transfers between devices  10.8 us (5%)
  other arithmetic  6.98 us (3%)
    all_gather x3, blocking collectives, per_device(): every_port = lax.all_gather(port_open, 'sub', axis=1, tiled=True)  92.5 us
    all_gather x1, waiting for transfers between devices, per_device(): full_inverse = lax.all_gather(internal_inverse, 'scen', axis=1, tiled=True)  43.5 us
    dot_general x3, matrix products, per_device(): jnp.einsum('sgm,gmn->sgn', injected, full_inverse, preferred_element_type...  15 us
    ppermute x2, starting transfers between devices, padded(): lax.ppermute(lax.slice_in_dim(block, block.shape[dim] - width, None, axis...  8.21 us
    dot_general x3, matrix products, per_device(): jnp.einsum('sgp,gpn->sgn', cable_in.reshape(scen_rows, slot_count, port_c...  6.85 us
    broadcast_in_dim x12, local copies, waits for them, and re-layouts, per_device(): jnp.where((lag_time == -delay_back)[None, :], hist_cols[delay_back], 0.0)  5.29 us
    convert_element_type x4, other arithmetic, per_device(): (port_used[None, :] * (0.5 * port_volt + cable_in)).astype(jnp.bfloat16)  4.8 us
  transfers between devices with their start and end apart: 5, of which 2 were waited for; matrix products, arithmetic and copies ran while one was open for 6% of the time, Pallas kernels for 0%

commit v1 on v0

--- a/solution.py
+++ b/solution.py
@@ -83,7 +83,15 @@
             "sgm,gmn->sgn", injected, full_inverse, preferred_element_type=jnp.float32
         )
         port_open = jnp.take_along_axis(opened, port_nodes[None], axis=2).reshape(scen_rows, if_dev)
-        every_port = lax.all_gather(port_open, "sub", axis=1, tiled=True)
+        ways, here = (lax.axis_size("sub"), lax.axis_index("sub"))
+        grown, reach = (port_open, 1)
+        while reach < ways:
+            theirs = lax.ppermute(grown, "sub", [(d, d ^ reach) for d in range(ways)])
+            mine_first = jnp.concatenate([grown, theirs], axis=1)
+            theirs_first = jnp.concatenate([theirs, grown], axis=1)
+            grown = jnp.where(here & reach == 0, mine_first, theirs_first)
+            reach = 2 * reach
+        every_port = grown
         link_current = lax.dot_general(
             every_port,
             schur_wide,

time: 229 us -> 183 us (0.80)
  blocking collectives: 92.5 us -> 0 us
  waiting for transfers between devices: 46.5 us -> 69.6 us
  starting transfers between devices: 10.8 us -> 31.6 us
    all_gather x3 -> x0, blocking collectives: 92.5 us -> none  [per_device(): every_port = lax.all_gather(port_open, 'sub', axis=1, tiled=True)]
    ppermute x0 -> x9, starting transfers between devices: none -> 20.5 us  [per_device(): theirs = lax.ppermute(grown, 'sub', [(d, d ^ reach) for d in range(ways)])]
    ppermute x0 -> x9, waiting for transfers between devices: none -> 17.6 us  [per_device(): theirs = lax.ppermute(grown, 'sub', [(d, d ^ reach) for d in range(ways)])]
    all_gather x1, waiting for transfers between devices: 43.5 us -> 49 us  [per_device(): full_inverse = lax.all_gather(internal_inverse, 'scen', axis=1, tiled=True)]
  transfers between devices with their start and end apart: 5 -> 14, of which waited for: 2 -> 10; matrix products, arithmetic and copies ran while one was open for 6% -> 10% of each run, Pallas kernels for 0% -> 0%
where the time goes in v1:
time: 183 us; the launch traced here: 182 us
  waiting for transfers between devices  69.6 us (38%)
  local copies, waits for them, and re-layouts  31.8 us (17%)
  starting transfers between devices  31.6 us (17%)
  matrix products  25.6 us (14%)
  between operations  15.6 us (9%)
  other arithmetic  8 us (4%)
    all_gather x1, waiting for transfers between devices, per_device(): full_inverse = lax.all_gather(internal_inverse, 'scen', axis=1, tiled=True)  49 us
    ppermute x9, starting transfers between devices, per_device(): theirs = lax.ppermute(grown, 'sub', [(d, d ^ reach) for d in range(ways)])  20.5 us
    ppermute x9, waiting for transfers between devices, per_device(): theirs = lax.ppermute(grown, 'sub', [(d, d ^ reach) for d in range(ways)])  17.6 us
    dot_general x3, matrix products, per_device(): jnp.einsum('sgm,gmn->sgn', injected, full_inverse, preferred_element_type...  15 us
    ppermute x2, starting transfers between devices, padded(): lax.ppermute(lax.slice_in_dim(block, block.shape[dim] - width, None, axis...  8.22 us
    dot_general x3, matrix products, per_device(): jnp.einsum('sgp,gpn->sgn', cable_in.reshape(scen_rows, slot_count, port_c...  6.89 us
    transpose x3, local copies, waits for them, and re-layouts, per_device(): jnp.einsum('sgm,gmn->sgn', injected, full_inverse, preferred_element_type...  5.76 us
    broadcast_in_dim x12, local copies, waits for them, and re-layouts, per_device(): jnp.where((lag_time == -delay_back)[None, :], hist_cols[delay_back], 0.0)  5.63 us
  transfers between devices with their start and end apart: 14, of which 10 were waited for; matrix products, arithmetic and copies ran while one was open for 10% of the time, Pallas kernels for 0%

profile of v1, /device:TPU:0, one launch (start us, length us, event | category | flops | bytes accessed | tf_op | source)
XLA Modules:
  0.0 182.1 jit_solution(15889680045200923253)
XLA Ops:
  7.3 0.7 all-gather.2.cloned.1.call-update
  8.2 4.8 %collective-permute-start = (bf16[4,64,64]{1,0,2:T(4,128)(2,1)S(1)}, bf16[4,64,64]{1,0,2:T(4,128)(2,1)S(1)}, u32[]{:S(2)}, u32[]{:S(2)}) collective-permute-start(bf16[4,64,64]{1,0,2:T(4,128)(2,1)S(1)} %copy.44), channel_id=1, source_target_pairs={{0,4},{4,8},{8,12},{12,16},{16,20},{20,24},{24,28},{1,5},{5,9},{9,... | collective-permute-start | bytes 98312 | tf_op jit(solution)/shard_map/ppermute | solution.py:15
  13.0 1.3 collective-permute-start.1
  15.0 0.6 compare_and_fusion.1
  16.9 2.3 %collective-permute-done.1 = bf16[4,64,64]{1,0,2:T(4,128)(2,1)S(1)} collective-permute-done((bf16[4,64,64]{1,0,2:T(4,128)(2,1)S(1)}, bf16[4,64,64]{1,0,2:T(4,128)(2,1)S(1)}, u32[]{:S(2)}, u32[]{:S(2)}) %collective-permute-start.1) | collective-permute-done | bytes 32800 | tf_op jit(solution)/shard_map/ppermute | solution.py:18
  19.4 0.7 gather_fusion
  20.3 1.3 fusion.12
  21.6 49.0 %all-gather.2.cloned.1.call-done = bf16[4,1024,1024]{2,1,0:T(8,128)(2,1)} async-done(((bf16[4,256,1024]{2,1,0:T(8,128)(2,1)}), bf16[4,1024,1024]{2,1,0:T(8,128)(2,1)}) %all-gather.2.cloned.1.call-update) | async-done | bytes 8388624 | tf_op jit(solution)/shard_map/all_gather | solution.py:57
  70.7 5.0 %convolution_bitcast_fusion.7 = f32[64,4,1024]{2,0,1:T(8,128)S(1)} fusion(bf16[64,4,1024]{2,0,1:T(8,128)(2,1)S(1)} %fusion.12, bf16[4,1024,1024]{2,1,0:T(8,128)(2,1)} %all-gather.2.cloned.1.call-done), kind=kOutput, calls=%fused_computation.29 | convolution fusion | flops 536870912 | bytes 9961472 | tf_op jit(solution)/shard_map/sgm,gmn->sgn/dot_general | solution.py:82
  75.8 1.9 %copy.47 = f32[64,4,1024]{0,2,1:T(8,128)} copy(f32[64,4,1024]{2,0,1:T(8,128)S(1)} %convolution_bitcast_fusion.7) | data formatting | bytes 2097152 | tf_op jit(solution)/shard_map/sgm,gmn->sgn/transpose | solution.py:82
  77.7 1.5 gather_fusion.3
  79.3 1.5 collective-permute-start.2
  80.8 2.4 %collective-permute-done.2 = f32[64,64]{0,1:T(8,128)S(1)} collective-permute-done((f32[64,64]{0,1:T(8,128)S(1)}, f32[64,64]{0,1:T(8,128)S(1)}, u32[]{:S(2)}, u32[]{:S(2)}) %collective-permute-start.2) | collective-permute-done | bytes 16416 | tf_op jit(solution)/shard_map/ppermute | solution.py:89
  83.2 1.6 collective-permute-start.3
  84.8 2.8 %collective-permute-done.3 = f32[64,128]{0,1:T(8,128)S(1)} collective-permute-done((f32[64,128]{0,1:T(8,128)S(1)}, f32[64,128]{0,1:T(8,128)S(1)}, u32[]{:S(2)}, u32[]{:S(2)}) %collective-permute-start.3) | collective-permute-done | bytes 32800 | tf_op jit(solution)/shard_map/ppermute | solution.py:89
  87.6 2.5 %collective-permute-start.4 = (f32[64,256]{0,1:T(8,128)S(1)}, f32[64,256]{0,1:T(8,128)S(1)}, u32[]{:S(2)}, u32[]{:S(2)}) collective-permute-start(f32[64,256]{0,1:T(8,128)S(1)} %maximum_select_fusion.6), channel_id=1, source_target_pairs={{0,16},{4,20},{8,24},{12,28},{16,0},{20,4},{24,8},{28,12},{1,17},{... | collective-permute-start | bytes 196616 | tf_op jit(solution)/shard_map/ppermute | solution.py:89
  90.2 0.6 mul.248
  90.8 1.8 gather_fusion.2
  92.6 2.3 %collective-permute-done.4 = f32[64,256]{0,1:T(8,128)S(1)} collective-permute-done((f32[64,256]{0,1:T(8,128)S(1)}, f32[64,256]{0,1:T(8,128)S(1)}, u32[]{:S(2)}, u32[]{:S(2)}) %collective-permute-start.4) | collective-permute-done | bytes 65568 | tf_op jit(solution)/shard_map/ppermute | solution.py:89
  96.4 0.9 gather_fusion.4
  97.4 0.9 fusion.63
  98.3 3.4 %collective-permute-start.5 = (bf16[64,64]{0,1:T(8,128)(2,1)S(1)}, bf16[64,64]{0,1:T(8,128)(2,1)S(1)}, u32[]{:S(2)}, u32[]{:S(2)}) collective-permute-start(bf16[64,64]{0,1:T(8,128)(2,1)S(1)} %fusion.63), channel_id=1, source_target_pairs={{0,4},{4,8},{8,12},{12,16},{16,20},{20,24},{24,28},{1,5},{5,9},{9,... | collective-permute-start | bytes 24584 | tf_op jit(solution)/shard_map/ppermute | solution.py:15
  101.7 1.5 collective-permute-start.6
  103.2 0.7 broadcast_multiply_fusion
  103.9 0.7 broadcast_in_dim.277
  104.6 0.7 broadcast_in_dim.267
  105.3 0.7 broadcast_in_dim.269
  106.0 0.7 broadcast_in_dim.271
  106.7 0.7 broadcast_in_dim.273
  107.4 0.7 broadcast_in_dim.275
  108.1 0.8 gather_fusion.1
  108.9 2.8 %fusion.13 = bf16[64,4,1024]{2,0,1:T(8,128)(2,1)S(1)} fusion(f32[64]{0:T(128)} %get-tuple-element.35, s32[4,1024]{1,0:T(4,128)} %copy-done.12, f32[4]{0:T(128)} %copy-done.18, s32[64]{0:T(128)} %param.22, f32[64,4,1024]{2,0,1:T(8,128)S(1)} %fusion.9, f32[4,1024]{1,0:T(4,128)S(1)} %broadcast_multiply_fusion, f32[64,4,1024]{2,1,0:T(4,128)} %param.20, ...), kind=kOutput, calls=%fused_computation.34 | convolution fusion | flops 52809728 | bytes 2729360 | tf_op jit(solution)/shard_map/sgp,gpn->sgn/dot_general | solution.py:73
  111.6 5.0 %convolution_bitcast_fusion.4 = f32[64,4,1024]{2,0,1:T(8,128)S(1)} fusion(bf16[64,4,1024]{2,0,1:T(8,128)(2,1)S(1)} %fusion.13, bf16[4,1024,1024]{2,1,0:T(8,128)(2,1)} %all-gather.2.cloned.1.call-done), kind=kOutput, calls=%fused_computation.22 | convolution fusion | flops 536870912 | bytes 9961472 | tf_op jit(solution)/shard_map/sgm,gmn->sgn/dot_general | solution.py:82
  116.7 1.9 %copy.50 = f32[64,4,1024]{0,2,1:T(8,128)} copy(f32[64,4,1024]{2,0,1:T(8,128)S(1)} %convolution_bitcast_fusion.4) | data formatting | bytes 2097152 | tf_op jit(solution)/shard_map/sgm,gmn->sgn/transpose | solution.py:82
  118.6 1.5 gather_fusion.5
  120.2 2.7 %collective-permute-start.7 = (f32[64,64]{0,1:T(8,128)S(1)}, f32[64,64]{0,1:T(8,128)S(1)}, u32[]{:S(2)}, u32[]{:S(2)}) collective-permute-start(f32[64,64]{0,1:T(8,128)S(1)} %bitcast.171), channel_id=1, source_target_pairs={{0,4},{4,0},{8,12},{12,8},{16,20},{20,16},{24,28},{28,24},{1,5},{5... | collective-permute-start | bytes 49160 | tf_op jit(solution)/shard_map/ppermute | solution.py:89
  122.9 1.9 %collective-permute-done.7 = f32[64,64]{0,1:T(8,128)S(1)} collective-permute-done((f32[64,64]{0,1:T(8,128)S(1)}, f32[64,64]{0,1:T(8,128)S(1)}, u32[]{:S(2)}, u32[]{:S(2)}) %collective-permute-start.7) | collective-permute-done | bytes 16416 | tf_op jit(solution)/shard_map/ppermute | solution.py:89
  124.8 2.0 %collective-permute-start.8 = (f32[64,128]{0,1:T(8,128)S(1)}, f32[64,128]{0,1:T(8,128)S(1)}, u32[]{:S(2)}, u32[]{:S(2)}) collective-permute-start(f32[64,128]{0,1:T(8,128)S(1)} %maximum_select_fusion.10), channel_id=1, source_target_pairs={{0,8},{4,12},{8,0},{12,4},{16,24},{20,28},{24,16},{28,20},{1,9},{5... | collective-permute-start | bytes 98312 | tf_op jit(solution)/shard_map/ppermute | solution.py:89
  126.8 2.8 %collective-permute-done.8 = f32[64,128]{0,1:T(8,128)S(1)} collective-permute-done((f32[64,128]{0,1:T(8,128)S(1)}, f32[64,128]{0,1:T(8,128)S(1)}, u32[]{:S(2)}, u32[]{:S(2)}) %collective-permute-start.8) | collective-permute-done | bytes 32800 | tf_op jit(solution)/shard_map/ppermute | solution.py:89
  129.6 3.2 %collective-permute-start.9 = (f32[64,256]{0,1:T(8,128)S(1)}, f32[64,256]{0,1:T(8,128)S(1)}, u32[]{:S(2)}, u32[]{:S(2)}) collective-permute-start(f32[64,256]{0,1:T(8,128)S(1)} %maximum_select_fusion.7), channel_id=1, source_target_pairs={{0,16},{4,20},{8,24},{12,28},{16,0},{20,4},{24,8},{28,12},{1,17},{... | collective-permute-start | bytes 196616 | tf_op jit(solution)/shard_map/ppermute | solution.py:89
  133.4 0.6 broadcast_in_dim.288
  134.7 0.7 broadcast_in_dim.292
  135.3 0.7 broadcast_in_dim.294
  136.4 0.7 copy.51
  137.2 1.1 fusion.5
  138.3 2.8 %fusion.14 = bf16[64,4,1024]{2,0,1:T(8,128)(2,1)S(1)} fusion(f32[64,4,1024]{2,0,1:T(8,128)S(1)} %fusion.5, f32[64]{0:T(128)} %get-tuple-element.33, s32[4,1024]{1,0:T(4,128)} %copy-done.12, f32[4,1024]{1,0:T(4,128)S(1)} %copy-done.14, f32[4]{0:T(128)} %copy-done.18, s32[64]{0:T(128)} %param.22, f32[64,4,1024]{2,0,1:T(8,128)S(1)} %fusion.9, ...), kind=kOutput, calls=%fused_computation.35 | convolution fusion | flops 53596160 | bytes 3777936 | tf_op jit(solution)/shard_map/sgp,gpn->sgn/dot_general | solution.py:73
  141.2 5.0 %convolution_bitcast_fusion.1 = f32[64,4,1024]{2,0,1:T(8,128)S(1)} fusion(bf16[64,4,1024]{2,0,1:T(8,128)(2,1)S(1)} %fusion.14, bf16[4,1024,1024]{2,1,0:T(8,128)(2,1)} %all-gather.2.cloned.1.call-done), kind=kOutput, calls=%fused_computation.15 | convolution fusion | flops 536870912 | bytes 9961472 | tf_op jit(solution)/shard_map/sgm,gmn->sgn/dot_general | solution.py:82
  146.2 1.9 %copy.52 = f32[64,4,1024]{0,2,1:T(8,128)} copy(f32[64,4,1024]{2,0,1:T(8,128)S(1)} %convolution_bitcast_fusion.1) | data formatting | bytes 2097152 | tf_op jit(solution)/shard_map/sgm,gmn->sgn/transpose | solution.py:82
  148.1 1.5 gather_fusion.6
  149.7 3.1 %collective-permute-start.10 = (f32[64,64]{0,1:T(8,128)S(1)}, f32[64,64]{0,1:T(8,128)S(1)}, u32[]{:S(2)}, u32[]{:S(2)}) collective-permute-start(f32[64,64]{0,1:T(8,128)S(1)} %bitcast.169), channel_id=1, source_target_pairs={{0,4},{4,0},{8,12},{12,8},{16,20},{20,16},{24,28},{28,24},{1,5},{5... | collective-permute-start | bytes 49160 | tf_op jit(solution)/shard_map/ppermute | solution.py:89
  152.8 1.9 %collective-permute-done.10 = f32[64,64]{0,1:T(8,128)S(1)} collective-permute-done((f32[64,64]{0,1:T(8,128)S(1)}, f32[64,64]{0,1:T(8,128)S(1)}, u32[]{:S(2)}, u32[]{:S(2)}) %collective-permute-start.10) | collective-permute-done | bytes 16416 | tf_op jit(solution)/shard_map/ppermute | solution.py:89
  154.7 1.5 collective-permute-start.11
  156.2 2.8 %collective-permute-done.11 = f32[64,128]{0,1:T(8,128)S(1)} collective-permute-done((f32[64,128]{0,1:T(8,128)S(1)}, f32[64,128]{0,1:T(8,128)S(1)}, u32[]{:S(2)}, u32[]{:S(2)}) %collective-permute-start.11) | collective-permute-done | bytes 32800 | tf_op jit(solution)/shard_map/ppermute | solution.py:89
  159.1 2.5 %collective-permute-start.12 = (f32[64,256]{0,1:T(8,128)S(1)}, f32[64,256]{0,1:T(8,128)S(1)}, u32[]{:S(2)}, u32[]{:S(2)}) collective-permute-start(f32[64,256]{0,1:T(8,128)S(1)} %maximum_select_fusion.8), channel_id=1, source_target_pairs={{0,16},{4,20},{8,24},{12,28},{16,0},{20,4},{24,8},{28,12},{1,17},{... | collective-permute-start | bytes 196616 | tf_op jit(solution)/shard_map/ppermute | solution.py:89
  161.6 0.7 multiply_convert_fusion.2
  162.3 1.9 %copy.54 = f32[64,4,1024]{0,2,1:T(8,128)} copy(f32[64,4,1024]{2,0,1:T(8,128)S(1)} %fusion.5) | data formatting | bytes 2097152 | tf_op jit(solution)/shard_map/mul | solution.py:106
  164.2 1.5 gather_fusion.7
  165.7 0.7 collective-permute-done.12
  166.9 1.1 fusion.121
  168.7 0.9 gather_fusion.8
  169.7 1.7 multiply_convert_fusion.1
  171.4 1.7 multiply_convert_fusion
  173.3 0.7 copy.59
  174.0 1.2 copy.58
  (154 shorter events, 6.9 us)
Async XLA Ops:
  7.2 87.7 %copy-start = (bf16[64,512]{1,0:T(8,128)(2,1)S(1)}, bf16[64,512]{1,0:T(8,128)(2,1)}, u32[]{:S(2)}) copy-start(bf16[64,512]{1,0:T(8,128)(2,1)} %param.14) | copy-start | bytes 196612
  7.2 7.8 %copy-start.51 = (s32[64]{0:T(128)S(1)}, s32[64]{0:T(128)}, u32[]{:S(2)}) copy-start(s32[64]{0:T(128)} %param.17) | copy-start | bytes 772
  7.2 7.8 %copy-start.52 = (s32[64]{0:T(128)S(1)}, s32[64]{0:T(128)}, u32[]{:S(2)}) copy-start(s32[64]{0:T(128)} %param.18) | copy-start | bytes 772
  7.2 8.5 %copy-start.50 = (f32[64]{0:T(128)S(1)}, f32[64]{0:T(128)}, u32[]{:S(2)}) copy-start(f32[64]{0:T(128)} %param.23) | copy-start | bytes 772
  7.2 9.1 %copy-start.16 = (s32[4,16]{1,0:T(4,128)S(1)}, s32[4,16]{1,0:T(4,128)}, u32[]{:S(2)}) copy-start(s32[4,16]{1,0:T(4,128)} %param.15) | copy-start | bytes 772
  7.2 13.1 %copy-start.2 = (f32[64,4,1024]{2,1,0:T(4,128)S(1)}, f32[64,4,1024]{2,1,0:T(4,128)}, u32[]{:S(2)}) copy-start(f32[64,4,1024]{2,1,0:T(4,128)} %param.20) | copy-start | bytes 3145732
  7.2 13.1 %copy-start.42 = (s32[64]{0:T(128)S(1)}, s32[64]{0:T(128)}, u32[]{:S(2)}) copy-start(s32[64]{0:T(128)} %param.22) | copy-start | bytes 772
  7.3 63.4 %all-gather.2.cloned.1.call-start = ((), (), s32[]{:S(2)}) async-start(), calls=%async_computation | async-start | bytes 10485760 | tf_op jit(solution)/shard_map/all_gather | solution.py:57
  8.2 8.8 %collective-permute-start = (bf16[4,64,64]{1,0,2:T(4,128)(2,1)S(1)}, bf16[4,64,64]{1,0,2:T(4,128)(2,1)S(1)}, u32[]{:S(2)}, u32[]{:S(2)}) collective-permute-start(bf16[4,64,64]{1,0,2:T(4,128)(2,1)S(1)} %copy.44), channel_id=1, source_target_pairs={{0,4},{4,8},{8,12},{12,16},{16,20},{20,24},{24,28},{1,5},{5,9},{9,... | collective-permute-start | bytes 98312 | tf_op jit(solution)/shard_map/ppermute | solution.py:15
  13.0 6.2 %collective-permute-start.1 = (bf16[4,64,64]{1,0,2:T(4,128)(2,1)S(1)}, bf16[4,64,64]{1,0,2:T(4,128)(2,1)S(1)}, u32[]{:S(2)}, u32[]{:S(2)}) collective-permute-start(bf16[4,64,64]{1,0,2:T(4,128)(2,1)S(1)} %copy.44), channel_id=1, source_target_pairs={{4,0},{8,4},{12,8},{16,12},{20,16},{24,20},{28,24},{5,1},{9,5},{13... | collective-permute-start | bytes 98312 | tf_op jit(solution)/shard_map/ppermute | solution.py:18
  15.6 1.2 copy-start.26
  15.6 60.0 %copy-start.20 = (pred[64]{0:T(512)(128)(4,1)}, pred[64]{0:T(512)(128)(4,1)S(1)}, u32[]{:S(2)}) copy-start(pred[64]{0:T(512)(128)(4,1)S(1)} %get-tuple-element.9) | copy-start | bytes 196
  15.6 60.0 %copy-start.28 = (pred[64]{0:T(512)(128)(4,1)}, pred[64]{0:T(512)(128)(4,1)S(1)}, u32[]{:S(2)}) copy-start(pred[64]{0:T(512)(128)(4,1)S(1)} %get-tuple-element.41) | copy-start | bytes 196
  15.6 60.1 %copy-start.30 = (pred[64]{0:T(512)(128)(4,1)}, pred[64]{0:T(512)(128)(4,1)S(1)}, u32[]{:S(2)}) copy-start(pred[64]{0:T(512)(128)(4,1)S(1)} %get-tuple-element.42) | copy-start | bytes 196
  15.7 60.1 %copy-start.32 = (pred[64]{0:T(512)(128)(4,1)}, pred[64]{0:T(512)(128)(4,1)S(1)}, u32[]{:S(2)}) copy-start(pred[64]{0:T(512)(128)(4,1)S(1)} %get-tuple-element.43) | copy-start | bytes 196
  15.7 60.0 %copy-start.25 = (s32[1024]{0:T(1024)}, s32[1024]{0:T(1024)S(1)}, u32[]{:S(2)}) copy-start(s32[1024]{0:T(1024)S(1)} %pad_clamp_fusion) | copy-start | bytes 12292
  16.4 59.3 %copy-start.12 = (s32[4,1024]{1,0:T(4,128)}, s32[4,1024]{1,0:T(4,128)S(1)}, u32[]{:S(2)}) copy-start(s32[4,1024]{1,0:T(4,128)S(1)} %iota_add_fusion) | copy-start | bytes 49156
  16.4 79.0 %copy-start.18 = (f32[4]{0:T(128)}, f32[4]{0:T(128)S(1)}, u32[]{:S(2)}) copy-start(f32[4]{0:T(128)S(1)} %compare_convert_fusion.1) | copy-start | bytes 52
  16.5 59.2 %copy-start.22 = (f32[4,16]{1,0:T(4,128)}, f32[4,16]{1,0:T(4,128)S(1)}, u32[]{:S(2)}) copy-start(f32[4,16]{1,0:T(4,128)S(1)} %mul.238) | copy-start | bytes 772
  20.3 55.5 %copy-start.3 = (f32[1,64,64]{1,0,2:T(1,128)}, f32[1,64,64]{1,0,2:T(1,128)S(1)}, u32[]{:S(2)}) copy-start(f32[1,64,64]{1,0,2:T(1,128)S(1)} %get-tuple-element.12) | copy-start | bytes 49156
  20.3 55.5 %copy-start.5 = (f32[1,64,64]{1,0,2:T(1,128)}, f32[1,64,64]{1,0,2:T(1,128)S(1)}, u32[]{:S(2)}) copy-start(f32[1,64,64]{1,0,2:T(1,128)S(1)} %get-tuple-element.13) | copy-start | bytes 49156
  20.3 55.5 %copy-start.6 = (f32[1,64,64]{1,0,2:T(1,128)}, f32[1,64,64]{1,0,2:T(1,128)S(1)}, u32[]{:S(2)}) copy-start(f32[1,64,64]{1,0,2:T(1,128)S(1)} %get-tuple-element.14) | copy-start | bytes 49156
  79.3 4.0 %collective-permute-start.2 = (f32[64,64]{0,1:T(8,128)S(1)}, f32[64,64]{0,1:T(8,128)S(1)}, u32[]{:S(2)}, u32[]{:S(2)}) collective-permute-start(f32[64,64]{0,1:T(8,128)S(1)} %bitcast.167), channel_id=1, source_target_pairs={{0,4},{4,0},{8,12},{12,8},{16,20},{20,16},{24,28},{28,24},{1,5},{5... | collective-permute-start | bytes 49160 | tf_op jit(solution)/shard_map/ppermute | solution.py:89
  83.2 4.3 %collective-permute-start.3 = (f32[64,128]{0,1:T(8,128)S(1)}, f32[64,128]{0,1:T(8,128)S(1)}, u32[]{:S(2)}, u32[]{:S(2)}) collective-permute-start(f32[64,128]{0,1:T(8,128)S(1)} %maximum_select_fusion.9), channel_id=1, source_target_pairs={{0,8},{4,12},{8,0},{12,4},{16,24},{20,28},{24,16},{28,20},{1,9},{5... | collective-permute-start | bytes 98312 | tf_op jit(solution)/shard_map/ppermute | solution.py:89
  87.6 7.3 %collective-permute-start.4 = (f32[64,256]{0,1:T(8,128)S(1)}, f32[64,256]{0,1:T(8,128)S(1)}, u32[]{:S(2)}, u32[]{:S(2)}) collective-permute-start(f32[64,256]{0,1:T(8,128)S(1)} %maximum_select_fusion.6), channel_id=1, source_target_pairs={{0,16},{4,20},{8,24},{12,28},{16,0},{20,4},{24,8},{28,12},{1,17},{... | collective-permute-start | bytes 196616 | tf_op jit(solution)/shard_map/ppermute | solution.py:89
  90.1 5.4 %copy-start.23 = (pred[4,16]{1,0:T(4,128)(4,1)}, pred[4,16]{1,0:T(4,128)(4,1)S(1)}, u32[]{:S(2)}) copy-start(pred[4,16]{1,0:T(4,128)(4,1)S(1)} %compare_and_fusion) | copy-start | bytes 196
  97.3 10.7 %copy-start.7 = (f32[64,4,16]{0,2,1:T(8,128)}, f32[64,4,16]{0,2,1:T(8,128)S(1)}, u32[]{:S(2)}) copy-start(f32[64,4,16]{0,2,1:T(8,128)S(1)} %bitcast_multiply_fusion.2) | copy-start | bytes 49156
  98.3 9.8 %collective-permute-start.5 = (bf16[64,64]{0,1:T(8,128)(2,1)S(1)}, bf16[64,64]{0,1:T(8,128)(2,1)S(1)}, u32[]{:S(2)}, u32[]{:S(2)}) collective-permute-start(bf16[64,64]{0,1:T(8,128)(2,1)S(1)} %fusion.63), channel_id=1, source_target_pairs={{0,4},{4,8},{8,12},{12,16},{16,20},{20,24},{24,28},{1,5},{5,9},{9,... | collective-permute-start | bytes 24584 | tf_op jit(solution)/shard_map/ppermute | solution.py:15
  101.7 6.4 %collective-permute-start.6 = (bf16[64,64]{0,1:T(8,128)(2,1)S(1)}, bf16[64,64]{0,1:T(8,128)(2,1)S(1)}, u32[]{:S(2)}, u32[]{:S(2)}) collective-permute-start(bf16[64,64]{0,1:T(8,128)(2,1)S(1)} %fusion.63), channel_id=1, source_target_pairs={{4,0},{8,4},{12,8},{16,12},{20,16},{24,20},{28,24},{5,1},{9,5},{13... | collective-permute-start | bytes 24584 | tf_op jit(solution)/shard_map/ppermute | solution.py:18
  103.9 12.7 %copy-start.13 = (f32[4,1024]{1,0:T(4,128)}, f32[4,1024]{1,0:T(4,128)S(1)}, u32[]{:S(2)}) copy-start(f32[4,1024]{1,0:T(4,128)S(1)} %broadcast_multiply_fusion) | copy-start | bytes 49156
  104.6 12.0 %copy-start.43 = (pred[4,16]{1,0:T(4,128)(4,1)}, pred[4,16]{1,0:T(4,128)(4,1)S(1)}, u32[]{:S(2)}) copy-start(pred[4,16]{1,0:T(4,128)(4,1)S(1)} %broadcast_in_dim.277) | copy-start | bytes 196
  108.9 7.8 %copy-start.9 = (bf16[64,64]{1,0:T(8,128)(2,1)}, bf16[64,64]{1,0:T(8,128)(2,1)S(1)}, u32[]{:S(2)}) copy-start(bf16[64,64]{1,0:T(8,128)(2,1)S(1)} %gather_fusion.1) | copy-start | bytes 24580
  116.7 16.1 %copy-start.41 = (pred[64]{0:T(512)(128)(4,1)S(1)}, pred[64]{0:T(512)(128)(4,1)}, u32[]{:S(2)}) copy-start(pred[64]{0:T(512)(128)(4,1)} %get-tuple-element.52) | copy-start | bytes 196
  116.7 16.8 %copy-start.40 = (pred[64]{0:T(512)(128)(4,1)S(1)}, pred[64]{0:T(512)(128)(4,1)}, u32[]{:S(2)}) copy-start(pred[64]{0:T(512)(128)(4,1)} %get-tuple-element.51) | copy-start | bytes 196
  116.7 17.4 %copy-start.38 = (pred[64]{0:T(512)(128)(4,1)S(1)}, pred[64]{0:T(512)(128)(4,1)}, u32[]{:S(2)}) copy-start(pred[64]{0:T(512)(128)(4,1)} %get-tuple-element.50) | copy-start | bytes 196
  116.7 18.0 %copy-start.36 = (pred[64]{0:T(512)(128)(4,1)S(1)}, pred[64]{0:T(512)(128)(4,1)}, u32[]{:S(2)}) copy-start(pred[64]{0:T(512)(128)(4,1)} %get-tuple-element.49) | copy-start | bytes 196
  116.7 18.7 %copy-start.34 = (pred[64]{0:T(512)(128)(4,1)S(1)}, pred[64]{0:T(512)(128)(4,1)}, u32[]{:S(2)}) copy-start(pred[64]{0:T(512)(128)(4,1)} %get-tuple-element.48) | copy-start | bytes 196
  118.6 19.6 %copy-start.4 = (f32[1,64,64]{1,0,2:T(1,128)S(1)}, f32[1,64,64]{1,0,2:T(1,128)}, u32[]{:S(2)}) copy-start(f32[1,64,64]{1,0,2:T(1,128)} %copy-done.3) | copy-start | bytes 49156
  120.2 4.6 %collective-permute-start.7 = (f32[64,64]{0,1:T(8,128)S(1)}, f32[64,64]{0,1:T(8,128)S(1)}, u32[]{:S(2)}, u32[]{:S(2)}) collective-permute-start(f32[64,64]{0,1:T(8,128)S(1)} %bitcast.171), channel_id=1, source_target_pairs={{0,4},{4,0},{8,12},{12,8},{16,20},{20,16},{24,28},{28,24},{1,5},{5... | collective-permute-start | bytes 49160 | tf_op jit(solution)/shard_map/ppermute | solution.py:89
  124.8 4.8 %collective-permute-start.8 = (f32[64,128]{0,1:T(8,128)S(1)}, f32[64,128]{0,1:T(8,128)S(1)}, u32[]{:S(2)}, u32[]{:S(2)}) collective-permute-start(f32[64,128]{0,1:T(8,128)S(1)} %maximum_select_fusion.10), channel_id=1, source_target_pairs={{0,8},{4,12},{8,0},{12,4},{16,24},{20,28},{24,16},{28,20},{1,9},{5... | collective-permute-start | bytes 98312 | tf_op jit(solution)/shard_map/ppermute | solution.py:89
  129.6 6.5 %collective-permute-start.9 = (f32[64,256]{0,1:T(8,128)S(1)}, f32[64,256]{0,1:T(8,128)S(1)}, u32[]{:S(2)}, u32[]{:S(2)}) collective-permute-start(f32[64,256]{0,1:T(8,128)S(1)} %maximum_select_fusion.7), channel_id=1, source_target_pairs={{0,16},{4,20},{8,24},{12,28},{16,0},{20,4},{24,8},{28,12},{1,17},{... | collective-permute-start | bytes 196616 | tf_op jit(solution)/shard_map/ppermute | solution.py:89
  137.1 1.2 copy-start.44
  137.1 1.2 copy-start.45
  137.1 1.2 copy-start.46
  137.1 1.2 copy-start.47
  137.1 1.2 copy-start.48
  137.2 1.2 copy-start.49
  146.2 15.4 %copy-start.8 = (f32[64,4,16]{0,2,1:T(8,128)S(1)}, f32[64,4,16]{0,2,1:T(8,128)}, u32[]{:S(2)}) copy-start(f32[64,4,16]{0,2,1:T(8,128)} %copy-done.7) | copy-start | bytes 49156
  146.2 15.4 %copy-start.17 = (f32[64]{0:T(128)S(1)}, f32[64]{0:T(128)}, u32[]{:S(2)}) copy-start(f32[64]{0:T(128)} %mul.248) | copy-start | bytes 772
  146.2 15.4 %copy-start.27 = (pred[64]{0:T(512)(128)(4,1)S(1)}, pred[64]{0:T(512)(128)(4,1)}, u32[]{:S(2)}) copy-start(pred[64]{0:T(512)(128)(4,1)} %copy-done.26) | copy-start | bytes 196
  146.2 15.4 %copy-start.29 = (pred[64]{0:T(512)(128)(4,1)S(1)}, pred[64]{0:T(512)(128)(4,1)}, u32[]{:S(2)}) copy-start(pred[64]{0:T(512)(128)(4,1)} %copy-done.28) | copy-start | bytes 196
  146.2 15.4 %copy-start.31 = (pred[64]{0:T(512)(128)(4,1)S(1)}, pred[64]{0:T(512)(128)(4,1)}, u32[]{:S(2)}) copy-start(pred[64]{0:T(512)(128)(4,1)} %copy-done.30) | copy-start | bytes 196
  146.2 15.4 %copy-start.33 = (pred[64]{0:T(512)(128)(4,1)S(1)}, pred[64]{0:T(512)(128)(4,1)}, u32[]{:S(2)}) copy-start(pred[64]{0:T(512)(128)(4,1)} %copy-done.32) | copy-start | bytes 196
  149.7 5.0 %collective-permute-start.10 = (f32[64,64]{0,1:T(8,128)S(1)}, f32[64,64]{0,1:T(8,128)S(1)}, u32[]{:S(2)}, u32[]{:S(2)}) collective-permute-start(f32[64,64]{0,1:T(8,128)S(1)} %bitcast.169), channel_id=1, source_target_pairs={{0,4},{4,0},{8,12},{12,8},{16,20},{20,16},{24,28},{28,24},{1,5},{5... | collective-permute-start | bytes 49160 | tf_op jit(solution)/shard_map/ppermute | solution.py:89
  154.7 4.3 %collective-permute-start.11 = (f32[64,128]{0,1:T(8,128)S(1)}, f32[64,128]{0,1:T(8,128)S(1)}, u32[]{:S(2)}, u32[]{:S(2)}) collective-permute-start(f32[64,128]{0,1:T(8,128)S(1)} %maximum_select_fusion.11), channel_id=1, source_target_pairs={{0,8},{4,12},{8,0},{12,4},{16,24},{20,28},{24,16},{28,20},{1,9},{5... | collective-permute-start | bytes 98312 | tf_op jit(solution)/shard_map/ppermute | solution.py:89
  159.1 7.3 %collective-permute-start.12 = (f32[64,256]{0,1:T(8,128)S(1)}, f32[64,256]{0,1:T(8,128)S(1)}, u32[]{:S(2)}, u32[]{:S(2)}) collective-permute-start(f32[64,256]{0,1:T(8,128)S(1)} %maximum_select_fusion.8), channel_id=1, source_target_pairs={{0,16},{4,20},{8,24},{12,28},{16,0},{20,4},{24,8},{28,12},{1,17},{... | collective-permute-start | bytes 196616 | tf_op jit(solution)/shard_map/ppermute | solution.py:89
  162.3 4.6 %copy-start.19 = (f32[4]{0:T(128)S(1)}, f32[4]{0:T(128)}, u32[]{:S(2)}) copy-start(f32[4]{0:T(128)} %copy-done.18) | copy-start | bytes 52
  162.3 4.6 %copy-start.24 = (pred[4,16]{1,0:T(4,128)(4,1)S(1)}, pred[4,16]{1,0:T(4,128)(4,1)}, u32[]{:S(2)}) copy-start(pred[4,16]{1,0:T(4,128)(4,1)} %copy-done.23) | copy-start | bytes 196
  168.1 1.6 copy-start.11
  168.1 1.6 copy-start.21
  168.1 3.3 %copy-start.35 = (pred[64]{0:T(512)(128)(4,1)S(1)}, pred[64]{0:T(512)(128)(4,1)}, u32[]{:S(2)}) copy-start(pred[64]{0:T(512)(128)(4,1)} %get-tuple-element.48) | copy-start | bytes 196
  168.1 3.3 %copy-start.37 = (pred[64]{0:T(512)(128)(4,1)S(1)}, pred[64]{0:T(512)(128)(4,1)}, u32[]{:S(2)}) copy-start(pred[64]{0:T(512)(128)(4,1)} %get-tuple-element.49) | copy-start | bytes 196
  168.1 3.3 %copy-start.39 = (pred[64]{0:T(512)(128)(4,1)S(1)}, pred[64]{0:T(512)(128)(4,1)}, u32[]{:S(2)}) copy-start(pred[64]{0:T(512)(128)(4,1)} %get-tuple-element.50) | copy-start | bytes 196
  168.7 5.3 %copy-start.1 = (bf16[64,4,1024]{2,0,1:T(8,128)(2,1)S(1)}, bf16[64,4,1024]{2,0,1:T(8,128)(2,1)}, u32[]{:S(2)}) copy-start(bf16[64,4,1024]{2,0,1:T(8,128)(2,1)} %get-tuple-element.37) | copy-start | bytes 1572868
  (3 other events, 3.1 us)
Sparse Core Ops, SparseCore 0:
  9.7 60.9 all-gather.1
